TPU v7x, 512 devices: a whole 4x8x8 slice. The times are simulated.
512 devices in a mesh: ctx: 16 (over y, core), head: 8 (over z), rep: 4 (over x).
Axes of the slice: x: 4, y: 8, z: 8, core: 2. Of those that a mesh axis runs over, the one named last changes fastest.
Arguments:
- q_turn: bfloat16 [1024, 8192], P(('rep', 'ctx', 'head')), parts along dimension 0, may hold values from -18 to 18
- k_turn: bfloat16 [1024, 1024], P(('rep', 'ctx', 'head')), parts along dimension 0, may hold values from -6 to 6
- v_turn: bfloat16 [1024, 1024], P(('rep', 'ctx', 'head')), parts along dimension 0, may hold values from -6 to 6
- cache_k: bfloat16 [2048, 64, 1024], P(('rep', 'ctx'), None, 'head'), parts along dimension 0, may hold values from -6 to 6
- cache_v: bfloat16 [2048, 64, 1024], P(('rep', 'ctx'), None, 'head'), parts along dimension 0, may hold values from -6 to 6
- k_scale: float32 [2048, 8], P(('rep', 'ctx'), 'head'), parts along dimension 0, may hold values from 0.25 to 2
- v_scale: float32 [2048, 8], P(('rep', 'ctx'), 'head'), parts along dimension 0, may hold values from 0.25 to 2
- page_map: int32 [2048], P(('rep', 'ctx')), parts along dimension 0, may hold values from 0 to 511, as said below
Outputs:
- attn_out: bfloat16 [1024, 8192], P(('rep', 'ctx'), 'head'), parts along dimension 0
- cache_k_paired: bfloat16 [131072, 1024], P(('rep', 'ctx'), 'head'), parts along dimension 0
- cache_v_paired: bfloat16 [131072, 1024], P(('rep', 'ctx'), 'head'), parts along dimension 0
There are 4 independent parts, one for each index of `rep`. A program takes and returns all parts, laid end to end along the dimension named above; each array names one. Nothing has to cross between parts.
Inputs may be any that keep to these rules, and one draw needn't show every extreme that they name: A permutation: slot s holds logical page page_map[s]. Cut the 512 logical pages into 32 blocks of 16 consecutive pages; the 32 slots of each index of ctx hold exactly one page of every block.
All inputs are finite; a program needn't handle non-finite values.
Results may differ from a plain program's by a relative error of at most 0.0087.
Values may be sent and summed in bfloat16 or wider, within the bound.
No kernel may reach another device: no remote copies, remote signals or barrier semaphores. Data moves between devices by JAX's collectives and lax.ppermute only.
A program may use at most 64 MiB of HBM per device.

v0:
```python
import math
import jax
import jax.numpy as jnp
from jax import lax
from jax.sharding import PartitionSpec as P


def sent_to_all(shard, axis):
    copies = jnp.broadcast_to(shard, (lax.axis_size(axis), *shard.shape))
    return lax.all_to_all(copies, axis, split_axis=0, concat_axis=0, tiled=True)


def joined_along(tiles, dim):
    lengths = list(tiles.shape[1:])
    lengths[dim] *= tiles.shape[0]
    return jnp.moveaxis(tiles, 0, dim).reshape(lengths)


def collect(shard, axis, dim):
    tiles = sent_to_all(shard, axis)
    return joined_along(tiles, dim)


def sent_together(arrays, axis, split_dim, concat_dim, along):
    both = jnp.concatenate(arrays, axis=along)
    whole, at, done = (
        lax.all_to_all(both, axis, split_axis=split_dim, concat_axis=concat_dim, tiled=True),
        0,
        [],
    )
    for a in arrays:
        done.append(lax.slice_in_dim(whole, at, at + a.shape[along], axis=along))
        at += a.shape[along]
    return tuple(done)


def scale_pages(codes, scales):
    slots, page_rows, width = codes.shape
    heads = scales.shape[1]
    full = (
        codes.astype(jnp.float32).reshape(slots, page_rows, heads, width // heads)
        * scales[:, None, :, None]
    )
    return full.reshape(slots, page_rows, width).astype(jnp.bfloat16)


def attend(queries, keys, values, turn_keys, turn_values, key_start, head_dim):
    length = queries.shape[0]
    q_heads = queries.shape[1] // head_dim
    kv_heads = keys.shape[1] // head_dim
    per_group = q_heads // kv_heads
    factor = 1.0 / math.sqrt(head_dim)
    by_head = queries.reshape(length, q_heads, head_dim).transpose(1, 0, 2)
    cache_kh = keys.reshape(keys.shape[0], kv_heads, head_dim)
    cache_vh = values.reshape(values.shape[0], kv_heads, head_dim)
    turn_kh = turn_keys.reshape(turn_keys.shape[0], kv_heads, head_dim)
    turn_vh = turn_values.reshape(turn_values.shape[0], kv_heads, head_dim)
    places = key_start + jnp.arange(turn_keys.shape[0], dtype=jnp.int32)
    visible = places[None, :] <= jnp.arange(length, dtype=jnp.int32)[:, None]
    dims = (((1,), (1,)), ((), ()))

    def one_head(pair):
        query, index = pair
        kv_index = index // per_group
        ck = lax.dynamic_index_in_dim(cache_kh, kv_index, 1, keepdims=False)
        cv = lax.dynamic_index_in_dim(cache_vh, kv_index, 1, keepdims=False)
        tk = lax.dynamic_index_in_dim(turn_kh, kv_index, 1, keepdims=False)
        tv = lax.dynamic_index_in_dim(turn_vh, kv_index, 1, keepdims=False)
        cached = lax.dot_general(query, ck, dims, preferred_element_type=jnp.float32) * factor
        recent = lax.dot_general(query, tk, dims, preferred_element_type=jnp.float32) * factor
        recent = jnp.where(visible, recent, -jnp.inf)
        peak = jnp.maximum(jnp.max(cached, axis=1), jnp.max(recent, axis=1))
        cached_e = jnp.exp(cached - peak[:, None])
        recent_e = jnp.exp(recent - peak[:, None])
        total = jnp.sum(cached_e, axis=1) + jnp.sum(recent_e, axis=1)
        mixed = jnp.dot(cached_e.astype(jnp.bfloat16), cv, preferred_element_type=jnp.float32)
        mixed = mixed + jnp.dot(
            recent_e.astype(jnp.bfloat16), tv, preferred_element_type=jnp.float32
        )
        return (mixed, peak, total)

    mixed, peak, total = lax.map(one_head, (by_head, jnp.arange(q_heads, dtype=jnp.int32)))
    return (mixed.transpose(1, 0, 2), peak.T, total.T)


def local(q_turn, k_turn, v_turn, cache_k, cache_v, k_scale, v_scale, page_map):
    ctx_count = lax.axis_size("ctx")
    position = lax.axis_index("ctx")
    slots, page_rows, width = cache_k.shape
    head_dim = width // k_scale.shape[1]
    half = slots // 2
    total_pages = slots * ctx_count
    per_peer = slots // ctx_count
    q_mine, k_mine, v_mine = (
        lax.all_to_all(q_turn, "head", split_axis=1, concat_axis=0, tiled=True),
        lax.all_to_all(k_turn, "head", split_axis=1, concat_axis=0, tiled=True),
        lax.all_to_all(v_turn, "head", split_axis=1, concat_axis=0, tiled=True),
    )
    queries = lax.all_gather(q_mine, "ctx", axis=0, tiled=True)
    own_rows = k_mine.shape[0]
    key_start = position * own_rows
    scaled_k = scale_pages(cache_k, k_scale)
    scaled_v = scale_pages(cache_v, v_scale)

    def owner_of(pages):
        block = pages // half
        return jnp.where(block < ctx_count, block, 2 * ctx_count - 1 - block)

    order = jnp.argsort(owner_of(page_map) * total_pages + page_map)
    send_k = scaled_k[order].reshape(slots * page_rows, width)
    send_v = scaled_v[order].reshape(slots * page_rows, width)
    every_map = collect(page_map, "ctx", 0)
    recv_k, recv_v = sent_together((send_k, send_v), "ctx", 0, 0, 1)
    maps = every_map.reshape(ctx_count, slots)
    mine = owner_of(maps) == position
    ranked = jnp.sort(jnp.where(mine, maps, maps + total_pages), axis=1)[:, :per_peer]
    arrived = ranked.reshape(slots)
    within = arrived % half
    place = jnp.where(arrived // half == position, within, half + within)
    back = jnp.argsort(place)
    paired_k = recv_k.reshape(slots, page_rows, width)[back].reshape(slots * page_rows, width)
    paired_v = recv_v.reshape(slots, page_rows, width)[back].reshape(slots * page_rows, width)
    mixed, peak, total = attend(
        queries,
        scaled_k.reshape(slots * page_rows, width),
        scaled_v.reshape(slots * page_rows, width),
        k_mine,
        v_mine,
        key_start,
        head_dim,
    )
    mixed_x, peak_x, total_x = (
        lax.all_to_all(mixed[:, None], "ctx", split_axis=0, concat_axis=1, tiled=True),
        lax.all_to_all(peak[:, None], "ctx", split_axis=0, concat_axis=1, tiled=True),
        lax.all_to_all(total[:, None], "ctx", split_axis=0, concat_axis=1, tiled=True),
    )
    peak_top = jnp.max(peak_x, axis=1)
    weights = jnp.exp(peak_x - peak_top[:, None])
    total_own = jnp.sum(total_x * weights, axis=1)
    mixed_own = jnp.sum(mixed_x * weights[..., None], axis=1)
    attn_out = (mixed_own / total_own[..., None]).reshape(own_rows, -1).astype(jnp.bfloat16)
    return (attn_out, paired_k, paired_v)


def solution(mesh):
    return jax.shard_map(
        local,
        mesh=mesh,
        in_specs=(
            P(("rep", "ctx", "head"), None),
            P(("rep", "ctx", "head"), None),
            P(("rep", "ctx", "head"), None),
            P(("rep", "ctx"), None, "head"),
            P(("rep", "ctx"), None, "head"),
            P(("rep", "ctx"), "head"),
            P(("rep", "ctx"), "head"),
            P(("rep", "ctx")),
        ),
        out_specs=(P(("rep", "ctx"), "head"), P(("rep", "ctx"), "head"), P(("rep", "ctx"), "head")),
        check_vma=False,
    )
```

profile of v0, /device:TPU:1, one launch (start us, length us, event | category | flops | bytes accessed | tf_op | source)
XLA Modules:
  0.0 218.2 jit_solution(17984911208036107442)
XLA Ops:
  0.6 10.9 %all-to-all-start = ((bf16[2,8,1024]{2,0,1:T(2,128)(2,1)}), bf16[2,8,1024]{2,0,1:T(2,128)(2,1)S(1)}, u32[]{:S(2)}, u32[]{:S(2)}) async-start(bf16[2,8,1024]{2,0,1:T(2,128)(2,1)} %bitcast.152), calls=%async_computation | async-start | bytes 65536 | tf_op jit(solution)/shard_map/all_to_all | solution.py:95
  12.2 1.2 multiply_convert_fusion
  13.4 1.2 multiply_convert_fusion.1
  14.6 1.6 sort.46
  16.2 2.2 all-to-all-done
  18.4 4.5 %all-to-all-start.2 = ((bf16[2,8,128]{2,0,1:T(2,128)(2,1)}), bf16[2,8,128]{2,0,1:T(2,128)(2,1)S(1)}, u32[]{:S(2)}, u32[]{:S(2)}) async-start(bf16[2,8,128]{2,0,1:T(2,128)(2,1)} %bitcast.11), calls=%async_computation.2 | async-start | bytes 8192 | tf_op jit(solution)/shard_map/all_to_all | solution.py:97
  22.9 6.4 %all-to-all-done.2 = bf16[2,8,128]{2,0,1:T(2,128)(2,1)S(1)} async-done(((bf16[2,8,128]{2,0,1:T(2,128)(2,1)}), bf16[2,8,128]{2,0,1:T(2,128)(2,1)S(1)}, u32[]{:S(2)}, u32[]{:S(2)}) %all-to-all-start.2) | async-done | bytes 4128 | tf_op jit(solution)/shard_map/all_to_all | solution.py:97
  29.4 3.3 %all-to-all-start.1 = ((bf16[2,8,128]{2,0,1:T(2,128)(2,1)}), bf16[2,8,128]{2,0,1:T(2,128)(2,1)S(1)}, u32[]{:S(2)}, u32[]{:S(2)}) async-start(bf16[2,8,128]{2,0,1:T(2,128)(2,1)} %bitcast.6), calls=%async_computation.1 | async-start | bytes 8192 | tf_op jit(solution)/shard_map/all_to_all | solution.py:96
  32.7 21.5 %all_gather.3 = bf16[256,1024]{1,0:T(8,128)(2,1)S(1)} all-gather(bf16[16,1024]{1,0:T(8,128)(2,1)S(1)} %all_to_all.92), channel_id=1, replica_groups=mesh['ctx'=16,'head'=8,'rep'=4] {'ctx'}, dimensions={0}, use_global_device_ids=true | all-gather | bytes 557056 | tf_op jit(solution)/shard_map/all_gather | solution.py:99
  54.2 1.0 copy.33
  55.8 4.5 %all-to-all-start.7 = ((s32[16,1,32]{2,1,0:T(1,128)}), s32[16,1,32]{2,1,0:T(1,128)S(1)}, u32[]{:S(2)}, u32[]{:S(2)}) async-start(s32[16,1,32]{2,1,0:T(1,128)} %broadcast_in_dim.50), calls=%async_computation.7 | async-start | bytes 16384 | tf_op jit(solution)/shard_map/all_to_all | solution.py:10
  60.3 66.8 %while.16 = (s32[]{:T(128)}, f32[8,256,128]{2,0,1:T(8,128)}, f32[8,256]{1,0:T(8,128)S(1)}, f32[8,256]{1,0:T(8,128)S(1)}, bf16[8,256,128]{1,2,0:T(8,128)(2,1)}, /...) while((s32[]{:T(128)}, f32[8,256,128]{2,0,1:T(8,128)}, ...), condition=%wide.region_5.6_spmd.clone, body=%wide.region_0.5_spmd.clone.sunk | while | flops 273743360 | bytes 8203457 | solution.py:82
  60.3 1.0 fusion.50
  61.3 1.4 fusion.51
  64.0 4.7 %dynamic_update_slice.20 = f32[8,256,128]{2,0,1:T(8,128)} dynamic-update-slice(f32[8,256,128]{2,0,1:T(8,128)} %get-tuple-element.254, f32[1,256,128]{2,0,1:T(1,128)S(1)} %bitcast.134, s32[]{:T(128)} %get-tuple-element.253, s32[]{:T(128)} %constant.101.clone.1..sunk, s32[]{:T(128)} %constant.101.clone.1..sunk) | dynamic-update-slice | bytes 262148 | tf_op jit(solution)/shard_map/while/body/jit(dynamic_update_index_in_dim)/dynamic_update_slice | solution.py:82
  68.7 1.0 fusion.50
  69.6 1.4 fusion.51
  72.3 4.7 %dynamic_update_slice.20 = f32[8,256,128]{2,0,1:T(8,128)} dynamic-update-slice(f32[8,256,128]{2,0,1:T(8,128)} %get-tuple-element.254, f32[1,256,128]{2,0,1:T(1,128)S(1)} %bitcast.134, s32[]{:T(128)} %get-tuple-element.253, s32[]{:T(128)} %constant.101.clone.1..sunk, s32[]{:T(128)} %constant.101.clone.1..sunk) | dynamic-update-slice | bytes 262148 | tf_op jit(solution)/shard_map/while/body/jit(dynamic_update_index_in_dim)/dynamic_update_slice | solution.py:82
  77.0 1.0 fusion.50
  78.0 1.4 fusion.51
  80.7 4.7 %dynamic_update_slice.20 = f32[8,256,128]{2,0,1:T(8,128)} dynamic-update-slice(f32[8,256,128]{2,0,1:T(8,128)} %get-tuple-element.254, f32[1,256,128]{2,0,1:T(1,128)S(1)} %bitcast.134, s32[]{:T(128)} %get-tuple-element.253, s32[]{:T(128)} %constant.101.clone.1..sunk, s32[]{:T(128)} %constant.101.clone.1..sunk) | dynamic-update-slice | bytes 262148 | tf_op jit(solution)/shard_map/while/body/jit(dynamic_update_index_in_dim)/dynamic_update_slice | solution.py:82
  85.4 1.0 fusion.50
  86.4 1.4 fusion.51
  89.0 4.7 %dynamic_update_slice.20 = f32[8,256,128]{2,0,1:T(8,128)} dynamic-update-slice(f32[8,256,128]{2,0,1:T(8,128)} %get-tuple-element.254, f32[1,256,128]{2,0,1:T(1,128)S(1)} %bitcast.134, s32[]{:T(128)} %get-tuple-element.253, s32[]{:T(128)} %constant.101.clone.1..sunk, s32[]{:T(128)} %constant.101.clone.1..sunk) | dynamic-update-slice | bytes 262148 | tf_op jit(solution)/shard_map/while/body/jit(dynamic_update_index_in_dim)/dynamic_update_slice | solution.py:82
  93.7 1.0 fusion.50
  94.7 1.4 fusion.51
  97.4 4.7 %dynamic_update_slice.20 = f32[8,256,128]{2,0,1:T(8,128)} dynamic-update-slice(f32[8,256,128]{2,0,1:T(8,128)} %get-tuple-element.254, f32[1,256,128]{2,0,1:T(1,128)S(1)} %bitcast.134, s32[]{:T(128)} %get-tuple-element.253, s32[]{:T(128)} %constant.101.clone.1..sunk, s32[]{:T(128)} %constant.101.clone.1..sunk) | dynamic-update-slice | bytes 262148 | tf_op jit(solution)/shard_map/while/body/jit(dynamic_update_index_in_dim)/dynamic_update_slice | solution.py:82
  102.1 1.0 fusion.50
  103.1 1.4 fusion.51
  105.7 4.7 %dynamic_update_slice.20 = f32[8,256,128]{2,0,1:T(8,128)} dynamic-update-slice(f32[8,256,128]{2,0,1:T(8,128)} %get-tuple-element.254, f32[1,256,128]{2,0,1:T(1,128)S(1)} %bitcast.134, s32[]{:T(128)} %get-tuple-element.253, s32[]{:T(128)} %constant.101.clone.1..sunk, s32[]{:T(128)} %constant.101.clone.1..sunk) | dynamic-update-slice | bytes 262148 | tf_op jit(solution)/shard_map/while/body/jit(dynamic_update_index_in_dim)/dynamic_update_slice | solution.py:82
  110.4 1.0 fusion.50
  111.4 1.4 fusion.51
  114.1 4.7 %dynamic_update_slice.20 = f32[8,256,128]{2,0,1:T(8,128)} dynamic-update-slice(f32[8,256,128]{2,0,1:T(8,128)} %get-tuple-element.254, f32[1,256,128]{2,0,1:T(1,128)S(1)} %bitcast.134, s32[]{:T(128)} %get-tuple-element.253, s32[]{:T(128)} %constant.101.clone.1..sunk, s32[]{:T(128)} %constant.101.clone.1..sunk) | dynamic-update-slice | bytes 262148 | tf_op jit(solution)/shard_map/while/body/jit(dynamic_update_index_in_dim)/dynamic_update_slice | solution.py:82
  118.8 1.0 fusion.50
  119.8 1.4 fusion.51
  122.5 4.7 %dynamic_update_slice.20 = f32[8,256,128]{2,0,1:T(8,128)} dynamic-update-slice(f32[8,256,128]{2,0,1:T(8,128)} %get-tuple-element.254, f32[1,256,128]{2,0,1:T(1,128)S(1)} %bitcast.134, s32[]{:T(128)} %get-tuple-element.253, s32[]{:T(128)} %constant.101.clone.1..sunk, s32[]{:T(128)} %constant.101.clone.1..sunk) | dynamic-update-slice | bytes 262148 | tf_op jit(solution)/shard_map/while/body/jit(dynamic_update_index_in_dim)/dynamic_update_slice | solution.py:82
  127.8 1.0 reduce.3
  129.5 7.2 %all-to-all-start.4 = ((f32[16,1,128]{2,1,0:T(1,128)}), f32[16,1,128]{2,1,0:T(1,128)S(1)}, u32[]{:S(2)}, u32[]{:S(2)}) async-start(f32[16,1,128]{2,1,0:T(1,128)} %reshape.187), calls=%async_computation.4 | async-start | bytes 16384 | tf_op jit(solution)/shard_map/all_to_all | solution.py:134
  138.2 1.0 reduce.1
  139.9 3.8 %all-to-all-done.4 = f32[16,1,128]{2,1,0:T(1,128)S(1)} async-done(((f32[16,1,128]{2,1,0:T(1,128)}), f32[16,1,128]{2,1,0:T(1,128)S(1)}, u32[]{:S(2)}, u32[]{:S(2)}) %all-to-all-start.4) | async-done | bytes 8224 | tf_op jit(solution)/shard_map/all_to_all | solution.py:134
  143.7 3.9 %all-to-all-start.5 = ((f32[16,1,128]{2,1,0:T(1,128)}), f32[16,1,128]{2,1,0:T(1,128)S(1)}, u32[]{:S(2)}, u32[]{:S(2)}) async-start(f32[16,1,128]{2,1,0:T(1,128)} %reshape.189), calls=%async_computation.5 | async-start | bytes 16384 | tf_op jit(solution)/shard_map/all_to_all | solution.py:135
  147.8 6.9 %all-to-all-done.5 = f32[16,1,128]{2,1,0:T(1,128)S(1)} async-done(((f32[16,1,128]{2,1,0:T(1,128)}), f32[16,1,128]{2,1,0:T(1,128)S(1)}, u32[]{:S(2)}, u32[]{:S(2)}) %all-to-all-start.5) | async-done | bytes 8224 | tf_op jit(solution)/shard_map/all_to_all | solution.py:135
  154.6 31.6 %all_to_all.123 = bf16[16,128,256]{2,1,0:T(8,128)(2,1)S(1)} all-to-all(bf16[16,128,256]{2,1,0:T(8,128)(2,1)S(1)} %pad_maximum_fusion), channel_id=1, replica_groups=mesh['ctx'=16,'head'=8,'rep'=4] {'ctx'}, dimensions={0} | all-to-all | bytes 2097152 | tf_op jit(solution)/shard_map/all_to_all | solution.py:27
  186.3 3.6 %all-to-all-start.3 = ((f32[256,1,8,128]{3,2,1,0:T(8,128)}), f32[256,1,8,128]{3,2,1,0:T(8,128)S(1)}, u32[]{:S(2)}, u32[]{:S(2)}) async-start(f32[256,1,8,128]{3,2,1,0:T(8,128)} %bitcast.15), calls=%async_computation.3 | async-start | bytes 2097152 | tf_op jit(solution)/shard_map/all_to_all | solution.py:133
  190.9 1.6 sort.48
  194.8 1.4 gather_fusion.2
  196.2 1.4 gather_fusion.3
  197.6 19.5 %all-to-all-done.3 = f32[256,1,8,128]{3,2,1,0:T(8,128)S(1)} async-done(((f32[256,1,8,128]{3,2,1,0:T(8,128)}), f32[256,1,8,128]{3,2,1,0:T(8,128)S(1)}, u32[]{:S(2)}, u32[]{:S(2)}) %all-to-all-start.3) | async-done | bytes 1048608 | tf_op jit(solution)/shard_map/all_to_all | solution.py:133
  (108 shorter events, 19.5 us)
Async XLA Ops:
  0.6 54.6 %copy-start = (s32[32]{0:T(128)S(1)}, s32[32]{0:T(128)}, u32[]{:S(2)}) copy-start(s32[32]{0:T(128)} %param.17) | copy-start | bytes 388
  0.6 17.7 %all-to-all-start = ((bf16[2,8,1024]{2,0,1:T(2,128)(2,1)}), bf16[2,8,1024]{2,0,1:T(2,128)(2,1)S(1)}, u32[]{:S(2)}, u32[]{:S(2)}) async-start(bf16[2,8,1024]{2,0,1:T(2,128)(2,1)} %bitcast.152), calls=%async_computation | async-start | bytes 65536 | tf_op jit(solution)/shard_map/all_to_all | solution.py:95
  18.4 11.0 %all-to-all-start.2 = ((bf16[2,8,128]{2,0,1:T(2,128)(2,1)}), bf16[2,8,128]{2,0,1:T(2,128)(2,1)S(1)}, u32[]{:S(2)}, u32[]{:S(2)}) async-start(bf16[2,8,128]{2,0,1:T(2,128)(2,1)} %bitcast.11), calls=%async_computation.2 | async-start | bytes 8192 | tf_op jit(solution)/shard_map/all_to_all | solution.py:97
  29.4 25.8 %all-to-all-start.1 = ((bf16[2,8,128]{2,0,1:T(2,128)(2,1)}), bf16[2,8,128]{2,0,1:T(2,128)(2,1)S(1)}, u32[]{:S(2)}, u32[]{:S(2)}) async-start(bf16[2,8,128]{2,0,1:T(2,128)(2,1)} %bitcast.6), calls=%async_computation.1 | async-start | bytes 8192 | tf_op jit(solution)/shard_map/all_to_all | solution.py:96
  55.8 73.7 %all-to-all-start.7 = ((s32[16,1,32]{2,1,0:T(1,128)}), s32[16,1,32]{2,1,0:T(1,128)S(1)}, u32[]{:S(2)}, u32[]{:S(2)}) async-start(s32[16,1,32]{2,1,0:T(1,128)} %broadcast_in_dim.50), calls=%async_computation.7 | async-start | bytes 16384 | tf_op jit(solution)/shard_map/all_to_all | solution.py:10
  129.5 14.2 %all-to-all-start.4 = ((f32[16,1,128]{2,1,0:T(1,128)}), f32[16,1,128]{2,1,0:T(1,128)S(1)}, u32[]{:S(2)}, u32[]{:S(2)}) async-start(f32[16,1,128]{2,1,0:T(1,128)} %reshape.187), calls=%async_computation.4 | async-start | bytes 16384 | tf_op jit(solution)/shard_map/all_to_all | solution.py:134
  143.7 10.9 %all-to-all-start.5 = ((f32[16,1,128]{2,1,0:T(1,128)}), f32[16,1,128]{2,1,0:T(1,128)S(1)}, u32[]{:S(2)}, u32[]{:S(2)}) async-start(f32[16,1,128]{2,1,0:T(1,128)} %reshape.189), calls=%async_computation.5 | async-start | bytes 16384 | tf_op jit(solution)/shard_map/all_to_all | solution.py:135
  186.3 30.9 %all-to-all-start.3 = ((f32[256,1,8,128]{3,2,1,0:T(8,128)}), f32[256,1,8,128]{3,2,1,0:T(8,128)S(1)}, u32[]{:S(2)}, u32[]{:S(2)}) async-start(f32[256,1,8,128]{3,2,1,0:T(8,128)} %bitcast.15), calls=%async_computation.3 | async-start | bytes 2097152 | tf_op jit(solution)/shard_map/all_to_all | solution.py:133
where the time goes:
time: 220 us; the launch traced here: 218 us
  blocking collectives  53.2 us (24%)
  local copies, waits for them, and re-layouts  46.7 us (21%)
  waiting for transfers between devices  38.8 us (18%)
  starting transfers between devices  37.9 us (17%)
  matrix products  24.9 us (11%)
  other arithmetic  15.5 us (7%)
    dynamic_update_slice x24, local copies, waits for them, and re-layouts, attend(): lax.map(one_head, (by_head, jnp.arange(q_heads, dtype=jnp.int32)))  37.8 us
    all_to_all x1, blocking collectives, sent_together(): lax.all_to_all(both, axis, split_axis=split_dim, concat_axis=concat_dim,...  31.6 us
    all_gather x1, blocking collectives, local(): queries = lax.all_gather(q_mine, 'ctx', axis=0, tiled=True)  21.5 us
    all_to_all x1, waiting for transfers between devices, local(): lax.all_to_all(mixed[:, None], 'ctx', split_axis=0, concat_axis=1, tiled=...  19.5 us
    dot_general x8, matrix products, one_head(): lax.dot_general(query, ck, dims, preferred_element_type=jnp.float32)  11.1 us
    all_to_all x1, starting transfers between devices, local(): lax.all_to_all(q_turn, 'head', split_axis=1, concat_axis=0, tiled=True)  10.9 us
    dot_general x8, matrix products, one_head(): lax.dot_general(query, tk, dims, preferred_element_type=jnp.float32)  7.9 us
    all_to_all x1, starting transfers between devices, local(): lax.all_to_all(peak[:, None], 'ctx', split_axis=0, concat_axis=1, tiled=T...  7.23 us
  transfers between devices with their start and end apart: 7, of which 5 were waited for; matrix products, arithmetic and copies ran while one was open for 39% of the time, Pallas kernels for 0%

commit v1 on v0

--- a/solution.py
+++ b/solution.py
@@ -96,7 +96,9 @@
         lax.all_to_all(k_turn, "head", split_axis=1, concat_axis=0, tiled=True),
         lax.all_to_all(v_turn, "head", split_axis=1, concat_axis=0, tiled=True),
     )
-    queries = lax.all_gather(q_mine, "ctx", axis=0, tiled=True)
+    queries = jnp.concatenate(
+        lax.all_to_all(jnp.stack([q_mine] * lax.axis_size("ctx")), "ctx", 0, 0), axis=0
+    )
     own_rows = k_mine.shape[0]
     key_start = position * own_rows
     scaled_k = scale_pages(cache_k, k_scale)

time: 220 us -> 231 us (1.050)
  waiting for transfers between devices: 38.8 us -> 55.9 us
  blocking collectives: 53.2 us -> 49.5 us
    all_gather x1 -> x0, blocking collectives: 21.5 us -> none  [local(): queries = lax.all_gather(q_mine, 'ctx', axis=0, tiled=True)]
    all_to_all x0 -> x1, blocking collectives: none -> 17.9 us  [local(): lax.all_to_all(q_turn, 'head', split_axis=1, concat_axis=0, tiled=True)]
    all_to_all x1, waiting for transfers between devices: 2.15 us -> 13.9 us  [local(): lax.all_to_all(jnp.stack([q_mine] * lax.axis_size('ctx')), 'ctx', 0, 0)]
    all_to_all x1, waiting for transfers between devices: 0.01 us -> 5.37 us  [local(): lax.all_to_all(k_turn, 'head', split_axis=1, concat_axis=0, tiled=True)]
  transfers between devices with their start and end apart: 7 -> 7, of which waited for: 5 -> 6; matrix products, arithmetic and copies ran while one was open for 39% -> 37% of each run, Pallas kernels for 0% -> 0%
where the time goes in v1:
time: 231 us; the launch traced here: 229 us
  waiting for transfers between devices  55.9 us (24%)
  blocking collectives  49.5 us (21%)
  local copies, waits for them, and re-layouts  47.6 us (21%)
  starting transfers between devices  35.8 us (15%)
  matrix products  24.6 us (11%)
  other arithmetic  14.1 us (6%)
    dynamic_update_slice x24, local copies, waits for them, and re-layouts, attend(): lax.map(one_head, (by_head, jnp.arange(q_heads, dtype=jnp.int32)))  37.8 us
    all_to_all x1, blocking collectives, sent_together(): lax.all_to_all(both, axis, split_axis=split_dim, concat_axis=concat_dim,...  31.6 us
    all_to_all x1, waiting for transfers between devices, local(): lax.all_to_all(mixed[:, None], 'ctx', split_axis=0, concat_axis=1, tiled=...  19.5 us
    all_to_all x1, blocking collectives, local(): lax.all_to_all(q_turn, 'head', split_axis=1, concat_axis=0, tiled=True)  17.9 us
    all_to_all x1, waiting for transfers between devices, local(): lax.all_to_all(jnp.stack([q_mine] * lax.axis_size('ctx')), 'ctx', 0, 0)  13.9 us
    dot_general x8, matrix products, one_head(): lax.dot_general(query, ck, dims, preferred_element_type=jnp.float32)  10.9 us
    all_to_all x1, starting transfers between devices, local(): lax.all_to_all(jnp.stack([q_mine] * lax.axis_size('ctx')), 'ctx', 0, 0)  10.4 us
    dot_general x8, matrix products, one_head(): lax.dot_general(query, tk, dims, preferred_element_type=jnp.float32)  8.04 us
  transfers between devices with their start and end apart: 7, of which 6 were waited for; matrix products, arithmetic and copies ran while one was open for 37% of the time, Pallas kernels for 0%

profile of v1, /device:TPU:1, one launch (start us, length us, event | category | flops | bytes accessed | tf_op | source)
XLA Modules:
  0.0 228.7 jit_solution(6597231359951751124)
XLA Ops:
  0.7 17.9 %all_to_all.125 = bf16[2,8,1024]{2,0,1:T(2,128)(2,1)S(1)} all-to-all(bf16[2,8,1024]{2,0,1:T(2,128)(2,1)} %bitcast.154), channel_id=1, replica_groups=mesh['ctx'=16,'head'=8,'rep'=4] {'head'}, dimensions={1} | all-to-all | bytes 65536 | tf_op jit(solution)/shard_map/all_to_all | solution.py:95
  18.5 3.3 %all-to-all-start.3 = ((bf16[2,8,128]{2,0,1:T(2,128)(2,1)}), bf16[2,8,128]{2,0,1:T(2,128)(2,1)S(1)}, u32[]{:S(2)}, u32[]{:S(2)}) async-start(bf16[2,8,128]{2,0,1:T(2,128)(2,1)} %bitcast.155), calls=%async_computation.3 | async-start | bytes 8192 | tf_op jit(solution)/shard_map/all_to_all | solution.py:97
  21.9 6.4 %all-to-all-done.3 = bf16[2,8,128]{2,0,1:T(2,128)(2,1)S(1)} async-done(((bf16[2,8,128]{2,0,1:T(2,128)(2,1)}), bf16[2,8,128]{2,0,1:T(2,128)(2,1)S(1)}, u32[]{:S(2)}, u32[]{:S(2)}) %all-to-all-start.3) | async-done | bytes 4128 | tf_op jit(solution)/shard_map/all_to_all | solution.py:97
  28.2 0.9 stack.5
  29.1 10.4 %all-to-all-start.1 = ((bf16[16,16,1024]{2,1,0:T(8,128)(2,1)}), bf16[16,16,1024]{2,1,0:T(8,128)(2,1)S(1)}, u32[]{:S(2)}, u32[]{:S(2)}) async-start(bf16[16,16,1024]{2,1,0:T(8,128)(2,1)} %stack.5), calls=%async_computation.1 | async-start | bytes 1048576 | tf_op jit(solution)/shard_map/all_to_all | solution.py:100
  40.1 1.6 sort.46
  42.8 13.9 %all-to-all-done.1 = bf16[16,16,1024]{2,1,0:T(8,128)(2,1)S(1)} async-done(((bf16[16,16,1024]{2,1,0:T(8,128)(2,1)}), bf16[16,16,1024]{2,1,0:T(8,128)(2,1)S(1)}, u32[]{:S(2)}, u32[]{:S(2)}) %all-to-all-start.1) | async-done | bytes 524320 | tf_op jit(solution)/shard_map/all_to_all | solution.py:100
  56.7 3.3 %all-to-all-start.2 = ((bf16[2,8,128]{2,0,1:T(2,128)(2,1)}), bf16[2,8,128]{2,0,1:T(2,128)(2,1)S(1)}, u32[]{:S(2)}, u32[]{:S(2)}) async-start(bf16[2,8,128]{2,0,1:T(2,128)(2,1)} %bitcast.5), calls=%async_computation.2 | async-start | bytes 8192 | tf_op jit(solution)/shard_map/all_to_all | solution.py:96
  60.1 0.9 copy.33
  61.0 5.4 %all-to-all-done.2 = bf16[2,8,128]{2,0,1:T(2,128)(2,1)S(1)} async-done(((bf16[2,8,128]{2,0,1:T(2,128)(2,1)}), bf16[2,8,128]{2,0,1:T(2,128)(2,1)S(1)}, u32[]{:S(2)}, u32[]{:S(2)}) %all-to-all-start.2) | async-done | bytes 4128 | tf_op jit(solution)/shard_map/all_to_all | solution.py:96
  67.0 4.1 %all-to-all-start.8 = ((s32[16,1,32]{2,1,0:T(1,128)}), s32[16,1,32]{2,1,0:T(1,128)S(1)}, u32[]{:S(2)}, u32[]{:S(2)}) async-start(s32[16,1,32]{2,1,0:T(1,128)} %broadcast_in_dim.50), calls=%async_computation.8 | async-start | bytes 16384 | tf_op jit(solution)/shard_map/all_to_all | solution.py:10
  71.1 66.5 %while.16 = (s32[]{:T(128)}, f32[8,256,128]{2,0,1:T(8,128)}, f32[8,256]{1,0:T(8,128)S(1)}, f32[8,256]{1,0:T(8,128)S(1)}, bf16[8,256,128]{2,1,0:T(8,128)(2,1)}, /...) while((s32[]{:T(128)}, f32[8,256,128]{2,0,1:T(8,128)}, ...), condition=%wide.region_5.6_spmd.clone, body=%wide.region_0.5_spmd.clone.sunk | while | flops 273743360 | bytes 8203457 | solution.py:82
  71.1 1.0 fusion.50
  72.1 1.4 fusion.51
  74.8 4.7 %dynamic_update_slice.20 = f32[8,256,128]{2,0,1:T(8,128)} dynamic-update-slice(f32[8,256,128]{2,0,1:T(8,128)} %get-tuple-element.254, f32[1,256,128]{2,0,1:T(1,128)S(1)} %bitcast.134, s32[]{:T(128)} %get-tuple-element.253, s32[]{:T(128)} %constant.101.clone.1..sunk, s32[]{:T(128)} %constant.101.clone.1..sunk) | dynamic-update-slice | bytes 262148 | tf_op jit(solution)/shard_map/while/body/jit(dynamic_update_index_in_dim)/dynamic_update_slice | solution.py:82
  79.5 1.0 fusion.50
  80.5 1.4 fusion.51
  83.1 4.7 %dynamic_update_slice.20 = f32[8,256,128]{2,0,1:T(8,128)} dynamic-update-slice(f32[8,256,128]{2,0,1:T(8,128)} %get-tuple-element.254, f32[1,256,128]{2,0,1:T(1,128)S(1)} %bitcast.134, s32[]{:T(128)} %get-tuple-element.253, s32[]{:T(128)} %constant.101.clone.1..sunk, s32[]{:T(128)} %constant.101.clone.1..sunk) | dynamic-update-slice | bytes 262148 | tf_op jit(solution)/shard_map/while/body/jit(dynamic_update_index_in_dim)/dynamic_update_slice | solution.py:82
  87.8 1.0 fusion.50
  88.8 1.4 fusion.51
  91.4 4.7 %dynamic_update_slice.20 = f32[8,256,128]{2,0,1:T(8,128)} dynamic-update-slice(f32[8,256,128]{2,0,1:T(8,128)} %get-tuple-element.254, f32[1,256,128]{2,0,1:T(1,128)S(1)} %bitcast.134, s32[]{:T(128)} %get-tuple-element.253, s32[]{:T(128)} %constant.101.clone.1..sunk, s32[]{:T(128)} %constant.101.clone.1..sunk) | dynamic-update-slice | bytes 262148 | tf_op jit(solution)/shard_map/while/body/jit(dynamic_update_index_in_dim)/dynamic_update_slice | solution.py:82
  96.1 1.0 fusion.50
  97.1 1.4 fusion.51
  99.7 4.7 %dynamic_update_slice.20 = f32[8,256,128]{2,0,1:T(8,128)} dynamic-update-slice(f32[8,256,128]{2,0,1:T(8,128)} %get-tuple-element.254, f32[1,256,128]{2,0,1:T(1,128)S(1)} %bitcast.134, s32[]{:T(128)} %get-tuple-element.253, s32[]{:T(128)} %constant.101.clone.1..sunk, s32[]{:T(128)} %constant.101.clone.1..sunk) | dynamic-update-slice | bytes 262148 | tf_op jit(solution)/shard_map/while/body/jit(dynamic_update_index_in_dim)/dynamic_update_slice | solution.py:82
  104.4 1.0 fusion.50
  105.4 1.4 fusion.51
  108.0 4.7 %dynamic_update_slice.20 = f32[8,256,128]{2,0,1:T(8,128)} dynamic-update-slice(f32[8,256,128]{2,0,1:T(8,128)} %get-tuple-element.254, f32[1,256,128]{2,0,1:T(1,128)S(1)} %bitcast.134, s32[]{:T(128)} %get-tuple-element.253, s32[]{:T(128)} %constant.101.clone.1..sunk, s32[]{:T(128)} %constant.101.clone.1..sunk) | dynamic-update-slice | bytes 262148 | tf_op jit(solution)/shard_map/while/body/jit(dynamic_update_index_in_dim)/dynamic_update_slice | solution.py:82
  112.7 1.0 fusion.50
  113.7 1.4 fusion.51
  116.3 4.7 %dynamic_update_slice.20 = f32[8,256,128]{2,0,1:T(8,128)} dynamic-update-slice(f32[8,256,128]{2,0,1:T(8,128)} %get-tuple-element.254, f32[1,256,128]{2,0,1:T(1,128)S(1)} %bitcast.134, s32[]{:T(128)} %get-tuple-element.253, s32[]{:T(128)} %constant.101.clone.1..sunk, s32[]{:T(128)} %constant.101.clone.1..sunk) | dynamic-update-slice | bytes 262148 | tf_op jit(solution)/shard_map/while/body/jit(dynamic_update_index_in_dim)/dynamic_update_slice | solution.py:82
  121.0 1.0 fusion.50
  122.0 1.4 fusion.51
  124.6 4.7 %dynamic_update_slice.20 = f32[8,256,128]{2,0,1:T(8,128)} dynamic-update-slice(f32[8,256,128]{2,0,1:T(8,128)} %get-tuple-element.254, f32[1,256,128]{2,0,1:T(1,128)S(1)} %bitcast.134, s32[]{:T(128)} %get-tuple-element.253, s32[]{:T(128)} %constant.101.clone.1..sunk, s32[]{:T(128)} %constant.101.clone.1..sunk) | dynamic-update-slice | bytes 262148 | tf_op jit(solution)/shard_map/while/body/jit(dynamic_update_index_in_dim)/dynamic_update_slice | solution.py:82
  129.3 1.0 fusion.50
  130.3 1.4 fusion.51
  133.0 4.7 %dynamic_update_slice.20 = f32[8,256,128]{2,0,1:T(8,128)} dynamic-update-slice(f32[8,256,128]{2,0,1:T(8,128)} %get-tuple-element.254, f32[1,256,128]{2,0,1:T(1,128)S(1)} %bitcast.134, s32[]{:T(128)} %get-tuple-element.253, s32[]{:T(128)} %constant.101.clone.1..sunk, s32[]{:T(128)} %constant.101.clone.1..sunk) | dynamic-update-slice | bytes 262148 | tf_op jit(solution)/shard_map/while/body/jit(dynamic_update_index_in_dim)/dynamic_update_slice | solution.py:82
  138.3 1.0 reduce.3
  140.0 7.2 %all-to-all-start.5 = ((f32[16,1,128]{2,1,0:T(1,128)}), f32[16,1,128]{2,1,0:T(1,128)S(1)}, u32[]{:S(2)}, u32[]{:S(2)}) async-start(f32[16,1,128]{2,1,0:T(1,128)} %reshape.186), calls=%async_computation.5 | async-start | bytes 16384 | tf_op jit(solution)/shard_map/all_to_all | solution.py:136
  148.7 1.0 reduce.1
  150.4 3.8 %all-to-all-done.5 = f32[16,1,128]{2,1,0:T(1,128)S(1)} async-done(((f32[16,1,128]{2,1,0:T(1,128)}), f32[16,1,128]{2,1,0:T(1,128)S(1)}, u32[]{:S(2)}, u32[]{:S(2)}) %all-to-all-start.5) | async-done | bytes 8224 | tf_op jit(solution)/shard_map/all_to_all | solution.py:136
  154.2 3.9 %all-to-all-start.6 = ((f32[16,1,128]{2,1,0:T(1,128)}), f32[16,1,128]{2,1,0:T(1,128)S(1)}, u32[]{:S(2)}, u32[]{:S(2)}) async-start(f32[16,1,128]{2,1,0:T(1,128)} %reshape.188), calls=%async_computation.6 | async-start | bytes 16384 | tf_op jit(solution)/shard_map/all_to_all | solution.py:137
  158.2 6.9 %all-to-all-done.6 = f32[16,1,128]{2,1,0:T(1,128)S(1)} async-done(((f32[16,1,128]{2,1,0:T(1,128)}), f32[16,1,128]{2,1,0:T(1,128)S(1)}, u32[]{:S(2)}, u32[]{:S(2)}) %all-to-all-start.6) | async-done | bytes 8224 | tf_op jit(solution)/shard_map/all_to_all | solution.py:137
  165.1 31.6 %all_to_all.126 = bf16[16,128,256]{2,1,0:T(8,128)(2,1)S(1)} all-to-all(bf16[16,128,256]{2,1,0:T(8,128)(2,1)S(1)} %pad_maximum_fusion), channel_id=1, replica_groups=mesh['ctx'=16,'head'=8,'rep'=4] {'ctx'}, dimensions={0} | all-to-all | bytes 2097152 | tf_op jit(solution)/shard_map/all_to_all | solution.py:27
  196.8 3.6 %all-to-all-start.4 = ((f32[256,1,8,128]{3,2,1,0:T(8,128)}), f32[256,1,8,128]{3,2,1,0:T(8,128)S(1)}, u32[]{:S(2)}, u32[]{:S(2)}) async-start(f32[256,1,8,128]{3,2,1,0:T(8,128)} %bitcast.14), calls=%async_computation.4 | async-start | bytes 2097152 | tf_op jit(solution)/shard_map/all_to_all | solution.py:135
  201.4 1.6 sort.48
  205.3 1.4 gather_fusion.2
  206.7 1.4 gather_fusion.3
  208.1 19.5 %all-to-all-done.4 = f32[256,1,8,128]{3,2,1,0:T(8,128)S(1)} async-done(((f32[256,1,8,128]{3,2,1,0:T(8,128)}), f32[256,1,8,128]{3,2,1,0:T(8,128)S(1)}, u32[]{:S(2)}, u32[]{:S(2)}) %all-to-all-start.4) | async-done | bytes 1048608 | tf_op jit(solution)/shard_map/all_to_all | solution.py:135
  (116 shorter events, 20.3 us)
Async XLA Ops:
  0.6 41.1 %copy-start = (bf16[32,64,128]{2,1,0:T(8,128)(2,1)S(1)}, bf16[32,64,128]{2,1,0:T(8,128)(2,1)}, u32[]{:S(2)}) copy-start(bf16[32,64,128]{2,1,0:T(8,128)(2,1)} %param.13) | copy-start | bytes 1572868
  0.6 42.0 %copy-start.2 = (f32[32,1]{0,1:T(1,128)S(1)}, f32[32,1]{0,1:T(1,128)}, u32[]{:S(2)}) copy-start(f32[32,1]{0,1:T(1,128)} %param.16) | copy-start | bytes 388
  0.7 42.0 %copy-start.1 = (bf16[32,64,128]{2,1,0:T(8,128)(2,1)S(1)}, bf16[32,64,128]{2,1,0:T(8,128)(2,1)}, u32[]{:S(2)}) copy-start(bf16[32,64,128]{2,1,0:T(8,128)(2,1)} %param.14) | copy-start | bytes 1572868
  18.5 9.7 %all-to-all-start.3 = ((bf16[2,8,128]{2,0,1:T(2,128)(2,1)}), bf16[2,8,128]{2,0,1:T(2,128)(2,1)S(1)}, u32[]{:S(2)}, u32[]{:S(2)}) async-start(bf16[2,8,128]{2,0,1:T(2,128)(2,1)} %bitcast.155), calls=%async_computation.3 | async-start | bytes 8192 | tf_op jit(solution)/shard_map/all_to_all | solution.py:97
  29.1 27.6 %all-to-all-start.1 = ((bf16[16,16,1024]{2,1,0:T(8,128)(2,1)}), bf16[16,16,1024]{2,1,0:T(8,128)(2,1)S(1)}, u32[]{:S(2)}, u32[]{:S(2)}) async-start(bf16[16,16,1024]{2,1,0:T(8,128)(2,1)} %stack.5), calls=%async_computation.1 | async-start | bytes 1048576 | tf_op jit(solution)/shard_map/all_to_all | solution.py:100
  41.8 24.6 %copy-start.3 = (s32[32]{0:T(128)S(1)}, s32[32]{0:T(128)}, u32[]{:S(2)}) copy-start(s32[32]{0:T(128)} %param.17) | copy-start | bytes 388
  56.7 9.7 %all-to-all-start.2 = ((bf16[2,8,128]{2,0,1:T(2,128)(2,1)}), bf16[2,8,128]{2,0,1:T(2,128)(2,1)S(1)}, u32[]{:S(2)}, u32[]{:S(2)}) async-start(bf16[2,8,128]{2,0,1:T(2,128)(2,1)} %bitcast.5), calls=%async_computation.2 | async-start | bytes 8192 | tf_op jit(solution)/shard_map/all_to_all | solution.py:96
  67.0 73.0 %all-to-all-start.8 = ((s32[16,1,32]{2,1,0:T(1,128)}), s32[16,1,32]{2,1,0:T(1,128)S(1)}, u32[]{:S(2)}, u32[]{:S(2)}) async-start(s32[16,1,32]{2,1,0:T(1,128)} %broadcast_in_dim.50), calls=%async_computation.8 | async-start | bytes 16384 | tf_op jit(solution)/shard_map/all_to_all | solution.py:10
  140.0 14.2 %all-to-all-start.5 = ((f32[16,1,128]{2,1,0:T(1,128)}), f32[16,1,128]{2,1,0:T(1,128)S(1)}, u32[]{:S(2)}, u32[]{:S(2)}) async-start(f32[16,1,128]{2,1,0:T(1,128)} %reshape.186), calls=%async_computation.5 | async-start | bytes 16384 | tf_op jit(solution)/shard_map/all_to_all | solution.py:136
  154.2 10.9 %all-to-all-start.6 = ((f32[16,1,128]{2,1,0:T(1,128)}), f32[16,1,128]{2,1,0:T(1,128)S(1)}, u32[]{:S(2)}, u32[]{:S(2)}) async-start(f32[16,1,128]{2,1,0:T(1,128)} %reshape.188), calls=%async_computation.6 | async-start | bytes 16384 | tf_op jit(solution)/shard_map/all_to_all | solution.py:137
  196.8 30.9 %all-to-all-start.4 = ((f32[256,1,8,128]{3,2,1,0:T(8,128)}), f32[256,1,8,128]{3,2,1,0:T(8,128)S(1)}, u32[]{:S(2)}, u32[]{:S(2)}) async-start(f32[256,1,8,128]{3,2,1,0:T(8,128)} %bitcast.14), calls=%async_computation.4 | async-start | bytes 2097152 | tf_op jit(solution)/shard_map/all_to_all | solution.py:135
